TPU v7x, 512 devices: a whole 4x4x16 slice. The times are simulated.
512 devices in a mesh: bis: 128 (over z, y, x_lo), src: 4 (over x_hi, core).
Axes of the slice: x: 4 (x_hi: 2, x_lo: 2; x = x_hi * 2 + x_lo), y: 4, z: 16, core: 2. Of those that a mesh axis runs over, the one named last changes fastest.
Arguments:
- coefficients: float32 [4, 2, 64, 32768], P('src', None, None, 'bis'), may hold values from -6 to 6
- factors: float32 [4, 3, 2048, 64, 256], P('src', None, 'bis'), may hold values from -0.375 to 0.375
Outputs:
- potentials: float32 [2, 64, 32768], P(None, 'src', 'bis')
All inputs are finite; a program needn't handle non-finite values.
Results may differ from a plain program's by a relative error of at most 0.0001.
Values sent between devices are 32-bit elements; how exact they have to be, the bound alone decides.
A program may use at most 64 MiB of HBM per device.

v0:
```python
import jax
import jax.numpy as jnp
from jax import lax
from jax.sharding import PartitionSpec as P

LEVELS = 3


def swapped(value, axis, stride):
    mask = 2**stride
    pairs = [(source, source ^ mask) for source in range(lax.axis_size(axis))]
    return lax.ppermute(value, axis, pairs)


def mix_blocks(factor, stacked):
    return jnp.einsum("boj,jbk->obk", factor, stacked, precision=lax.Precision.HIGHEST)


def advance(state, factor, bit):
    real_part = state[0]
    imag_part = state[1]
    partner = swapped(state, "bis", bit)
    other_re = partner[0]
    other_im = partner[1]
    stack_re = jnp.concatenate([real_part, -imag_part, other_re, -other_im], axis=0)
    stack_im = jnp.concatenate([imag_part, real_part, other_im, other_re], axis=0)
    new_re = mix_blocks(factor, stack_re)
    new_im = mix_blocks(factor, stack_im)
    return jnp.stack([new_re, new_im], axis=0)


def per_device(coefficients, factors):
    middle = (lax.axis_size("bis").bit_length() - 1) // 2
    rank = coefficients.shape[2]
    columns = coefficients.shape[3]
    blocks = factors.shape[2]
    state = coefficients[0].reshape(2, rank, blocks, columns // blocks)
    for level_num in range(LEVELS):
        state = advance(state, factors[0, level_num], middle + 1 - level_num)
    flat = state.reshape(2, rank, columns)
    total = lax.psum(flat, "src")
    share = rank // lax.axis_size("src")
    start = lax.axis_index("src") * share
    return lax.dynamic_slice_in_dim(total, start, share, 1)


def solution(mesh):
    placed = (P("src", None, None, "bis"), P("src", None, "bis", None, None))
    return jax.shard_map(
        per_device, mesh=mesh, in_specs=placed, out_specs=P(None, "src", "bis"), check_vma=False
    )
```

profile of v0, /device:TPU:1, one launch (start us, length us, event | category | flops | bytes accessed | tf_op | source)
XLA Modules:
  0.0 131.5 jit_solution(13678017385581789084)
XLA Ops:
  6.5 1.9 %copy.5 = f32[1,2,64,256]{2,3,1,0:T(8,128)} copy(f32[1,2,64,256]{3,2,1,0:T(8,128)} %param.2) | data formatting | bytes 262144 | tf_op args[0]
  8.4 5.7 %collective-permute-start = (f32[2,64,16,16]{1,3,2,0:T(8,128)}, f32[2,64,16,16]{1,3,2,0:T(8,128)}, u32[]{:S(2)}, u32[]{:S(2)}) collective-permute-start(f32[2,64,16,16]{1,3,2,0:T(8,128)} %bitcast.2), channel_id=1, source_target_pairs={{0,64},{4,68},{8,72},{12,76},{16,80},{20,84},{24,88},{28,92},{32,9... | collective-permute-start | bytes 393224 | tf_op jit(solution)/shard_map/ppermute | solution.py:12
  14.2 1.5 %fusion.69 = (f32[1,1,64,256]{3,2,1,0:T(8,128)S(1)}, f32[1,1,64,256]{3,2,1,0:T(8,128)}) fusion(f32[1,2,64,256]{3,2,1,0:T(8,128)} %param.2), kind=kLoop, calls=%fused_computation.81 | loop fusion | bytes 262144 | tf_op jit(solution)/shard_map/slice | solution.py:21
  15.8 0.9 copy.3
  16.7 8.7 %collective-permute-done = f32[2,64,16,16]{1,3,2,0:T(8,128)} collective-permute-done((f32[2,64,16,16]{1,3,2,0:T(8,128)}, f32[2,64,16,16]{1,3,2,0:T(8,128)}, u32[]{:S(2)}, u32[]{:S(2)}) %collective-permute-start) | collective-permute-done | bytes 131104 | tf_op jit(solution)/shard_map/ppermute | solution.py:12
  25.4 1.0 slice_bitcast_fusion.4
  26.4 2.3 %bitcast_negate_fusion.1 = (f32[64,16,16]{0,2,1:T(8,128)S(1)}, f32[16,16,64]{2,1,0:T(8,128)S(1)}) fusion(f32[1,3,16,64,256]{4,3,2,1,0:T(8,128)} %param.3, f32[64,16,16]{0,2,1:T(8,128)S(1)} %get-tuple-element.10, f32[64,16,16]{0,2,1:T(8,128)S(1)} %get-tuple-element.9, f32[64,16,16]{0,2,1:T(8,128)S(1)} %bitcast.70, f32[64,16,16]{0,2,1:T(8,128)S(1)} %bitcast.69), kind=kOutput, calls=%fused_computation.77 | convolution fusion | flops 50544640 | bytes 1441792 | tf_op jit(solution)/shard_map/boj,jbk->obk/dot_general | solution.py:16
  28.7 0.9 fusion.66
  29.6 1.1 fusion.10
  30.7 3.8 %collective-permute-start.1 = (f32[2,64,16,16]{1,3,2,0:T(8,128)S(1)}, f32[2,64,16,16]{1,3,2,0:T(8,128)S(1)}, u32[]{:S(2)}, u32[]{:S(2)}) collective-permute-start(f32[2,64,16,16]{1,3,2,0:T(8,128)S(1)} %pad_maximum_fusion), channel_id=1, source_target_pairs={{0,32},{4,36},{8,40},{12,44},{16,48},{20,52},{24,56},{28,60},{32,0... | collective-permute-start | bytes 393224 | tf_op jit(solution)/shard_map/ppermute | solution.py:12
  34.5 5.2 %collective-permute-done.1 = f32[2,64,16,16]{1,3,2,0:T(8,128)S(1)} collective-permute-done((f32[2,64,16,16]{1,3,2,0:T(8,128)S(1)}, f32[2,64,16,16]{1,3,2,0:T(8,128)S(1)}, u32[]{:S(2)}, u32[]{:S(2)}) %collective-permute-start.1) | collective-permute-done | bytes 131104 | tf_op jit(solution)/shard_map/ppermute | solution.py:12
  39.7 1.1 fusion.6
  40.7 1.1 bitcast_negate_fusion
  41.8 5.0 %collective-permute-start.2 = (f32[2,64,16,16]{1,3,2,0:T(8,128)S(1)}, f32[2,64,16,16]{1,3,2,0:T(8,128)S(1)}, u32[]{:S(2)}, u32[]{:S(2)}) collective-permute-start(f32[2,64,16,16]{1,3,2,0:T(8,128)S(1)} %pad_maximum_fusion.1), channel_id=1, source_target_pairs={{0,16},{4,20},{8,24},{12,28},{16,0},{20,4},{24,8},{28,12},{32,48},... | collective-permute-start | bytes 393224 | tf_op jit(solution)/shard_map/ppermute | solution.py:12
  46.9 4.4 %collective-permute-done.2 = f32[2,64,16,16]{1,3,2,0:T(8,128)S(1)} collective-permute-done((f32[2,64,16,16]{1,3,2,0:T(8,128)S(1)}, f32[2,64,16,16]{1,3,2,0:T(8,128)S(1)}, u32[]{:S(2)}, u32[]{:S(2)}) %collective-permute-start.2) | collective-permute-done | bytes 131104 | tf_op jit(solution)/shard_map/ppermute | solution.py:12
  51.3 0.7 copy-done.1
  52.0 1.7 %fusion = f32[16,16,64]{2,1,0:T(8,128)} fusion(f32[1,3,16,64,256]{4,3,2,1,0:T(8,128)S(1)} %copy-done, f32[64,16,16]{0,2,1:T(8,128)S(1)} %get-tuple-element.6, f32[64,16,16]{0,2,1:T(8,128)S(1)} %get-tuple-element.5, f32[64,16,16]{0,2,1:T(8,128)S(1)} %bitcast.64, f32[64,16,16]{0,2,1:T(8,128)S(1)} %bitcast.73), kind=kOutput, calls=%fused_computation | convolution fusion | flops 50528256 | bytes 1638400 | tf_op jit(solution)/shard_map/boj,jbk->obk/dot_general | solution.py:16
  53.7 1.6 %copy.7 = f32[1,64,256]{2,1,0:T(8,128)} copy(f32[1,64,256]{1,2,0:T(8,128)} %bitcast.75) | data formatting | bytes 131072 | tf_op jit(solution)/shard_map/stack | solution.py:29
  55.3 0.9 fusion.68
  56.3 1.7 %fusion.2 = f32[16,16,64]{2,1,0:T(8,128)} fusion(f32[1,3,16,64,256]{4,3,2,1,0:T(8,128)S(1)} %copy-done, f32[64,16,16]{0,2,1:T(8,128)S(1)} %fusion.68, f32[64,16,16]{0,2,1:T(8,128)S(1)} %get-tuple-element.6, f32[64,16,16]{0,2,1:T(8,128)S(1)} %get-tuple-element.15, f32[64,16,16]{0,2,1:T(8,128)S(1)} %bitcast.65), kind=kOutput, calls=%fused_computation.2 | convolution fusion | flops 50528256 | bytes 1638400 | tf_op jit(solution)/shard_map/boj,jbk->obk/dot_general | solution.py:16
  58.0 1.0 copy.6
  59.0 1.5 %pad_maximum_fusion.2 = f32[2,64,256]{2,1,0:T(8,128)} fusion(f32[1,64,256]{2,1,0:T(8,128)} %copy.7, f32[1,64,256]{2,1,0:T(8,128)S(1)} %copy.6), kind=kLoop, calls=%fused_computation.68 | loop fusion | flops 32768 | bytes 262144 | tf_op jit(solution)/shard_map/stack | solution.py:29
  60.5 62.8 %all-reduce.2.cloned.1.call-done = f32[2,64,256]{2,1,0:T(8,128)} async-done(((f32[2,64,256]{2,1,0:T(8,128)}), f32[2,64,256]{2,1,0:T(8,128)}) %all-reduce.2.cloned.1.call-update) | async-done | bytes 131088 | tf_op jit(solution)/shard_map/psum | solution.py:41
  123.3 1.4 %constant_dynamic-slice_fusion = f32[2,16,256]{2,1,0:T(8,128)} fusion(f32[2,64,256]{2,1,0:T(8,128)} %all-reduce.2.cloned.1.call-done, s32[]{:T(128)S(6)} %select_n.3), kind=kLoop, calls=%fused_computation.69 | loop fusion | bytes 65540 | tf_op jit(solution)/shard_map/dynamic_slice | solution.py:44
  (12 shorter events, 0.2 us)
Async XLA Ops:
  6.5 23.1 %copy-start = (f32[1,3,16,64,256]{4,3,2,1,0:T(8,128)S(1)}, f32[1,3,16,64,256]{4,3,2,1,0:T(8,128)}, u32[]{:S(2)}) copy-start(f32[1,3,16,64,256]{4,3,2,1,0:T(8,128)} %param.3) | copy-start | bytes 9437188
  6.5 116.7 %all-reduce.2.cloned.1.call-start = ((), (), s32[]{:S(2)}) async-start(), calls=%async_computation | async-start | bytes 262144 | tf_op jit(solution)/shard_map/psum | solution.py:41
  8.4 17.0 %collective-permute-start = (f32[2,64,16,16]{1,3,2,0:T(8,128)}, f32[2,64,16,16]{1,3,2,0:T(8,128)}, u32[]{:S(2)}, u32[]{:S(2)}) collective-permute-start(f32[2,64,16,16]{1,3,2,0:T(8,128)} %bitcast.2), channel_id=1, source_target_pairs={{0,64},{4,68},{8,72},{12,76},{16,80},{20,84},{24,88},{28,92},{32,9... | collective-permute-start | bytes 393224 | tf_op jit(solution)/shard_map/ppermute | solution.py:12
  30.7 8.9 %collective-permute-start.1 = (f32[2,64,16,16]{1,3,2,0:T(8,128)S(1)}, f32[2,64,16,16]{1,3,2,0:T(8,128)S(1)}, u32[]{:S(2)}, u32[]{:S(2)}) collective-permute-start(f32[2,64,16,16]{1,3,2,0:T(8,128)S(1)} %pad_maximum_fusion), channel_id=1, source_target_pairs={{0,32},{4,36},{8,40},{12,44},{16,48},{20,52},{24,56},{28,60},{32,0... | collective-permute-start | bytes 393224 | tf_op jit(solution)/shard_map/ppermute | solution.py:12
  41.8 9.5 %collective-permute-start.2 = (f32[2,64,16,16]{1,3,2,0:T(8,128)S(1)}, f32[2,64,16,16]{1,3,2,0:T(8,128)S(1)}, u32[]{:S(2)}, u32[]{:S(2)}) collective-permute-start(f32[2,64,16,16]{1,3,2,0:T(8,128)S(1)} %pad_maximum_fusion.1), channel_id=1, source_target_pairs={{0,16},{4,20},{8,24},{12,28},{16,0},{20,4},{24,8},{28,12},{32,48},... | collective-permute-start | bytes 393224 | tf_op jit(solution)/shard_map/ppermute | solution.py:12
  51.3 0.7 copy-start.1
Sparse Core Ops, SparseCore 0:
  60.6 62.6 all-reduce.1
where the time goes:
time: 132 us; the launch traced here: 131 us
  waiting for transfers between devices  81.1 us (61%)
  starting transfers between devices  14.5 us (11%)
  between operations  13.5 us (10%)
  local copies, waits for them, and re-layouts  10.1 us (8%)
  matrix products  8.87 us (7%)
  other arithmetic  3.4 us (3%)
    psum x1, waiting for transfers between devices, per_device(): total = lax.psum(flat, 'src')  62.8 us
    ppermute x3, waiting for transfers between devices, swapped(): return lax.ppermute(value, axis, pairs)  18.3 us
    ppermute x3, starting transfers between devices, swapped(): return lax.ppermute(value, axis, pairs)  14.5 us
    dot_general x6, matrix products, mix_blocks(): jnp.einsum('boj,jbk->obk', factor, stacked, precision=lax.Precision.HIGHEST)  8.87 us
  transfers between devices with their start and end apart: 4, of which 4 were waited for; matrix products, arithmetic and copies ran while one was open for 2% of the time, Pallas kernels for 0%

commit v1 on v0

--- a/solution.py
+++ b/solution.py
@@ -38,7 +38,7 @@
     for level_num in range(LEVELS):
         state = advance(state, factors[0, level_num], middle + 1 - level_num)
     flat = state.reshape(2, rank, columns)
-    total = lax.psum(flat, "src")
+    total = jnp.sum(lax.all_gather(flat, "src"), axis=0)
     share = rank // lax.axis_size("src")
     start = lax.axis_index("src") * share
     return lax.dynamic_slice_in_dim(total, start, share, 1)

time: 132 us -> 68.8 us (0.52)
  waiting for transfers between devices: 81.1 us -> 18.6 us
  between operations: 13.5 us -> 0.11 us
  blocking collectives: 0 us -> 11.4 us
  matrix products: 8.87 us -> 10.4 us
    psum x1 -> x0, waiting for transfers between devices: 62.8 us -> none  [per_device(): total = lax.psum(flat, 'src')]
    all_gather x0 -> x1, blocking collectives: none -> 11.4 us  [per_device(): total = jnp.sum(lax.all_gather(flat, 'src'), axis=0)]
    dot_general x6, matrix products: 8.87 us -> 10.4 us  [mix_blocks(): jnp.einsum('boj,jbk->obk', factor, stacked, precision=lax.Precision.HIGHEST)]
  transfers between devices with their start and end apart: 4 -> 3, of which waited for: 4 -> 3; matrix products, arithmetic and copies ran while one was open for 2% -> 4% of each run, Pallas kernels for 0% -> 0%
where the time goes in v1:
time: 68.8 us; the launch traced here: 68.2 us
  waiting for transfers between devices  18.6 us (27%)
  starting transfers between devices  14.5 us (21%)
  blocking collectives  11.4 us (17%)
  matrix products  10.4 us (15%)
  local copies, waits for them, and re-layouts  9.62 us (14%)
  other arithmetic  3.49 us (5%)
    ppermute x3, waiting for transfers between devices, swapped(): return lax.ppermute(value, axis, pairs)  18.6 us
    ppermute x3, starting transfers between devices, swapped(): return lax.ppermute(value, axis, pairs)  14.5 us
    all_gather x1, blocking collectives, per_device(): total = jnp.sum(lax.all_gather(flat, 'src'), axis=0)  11.4 us
    dot_general x6, matrix products, mix_blocks(): jnp.einsum('boj,jbk->obk', factor, stacked, precision=lax.Precision.HIGHEST)  10.4 us
    another operation x2, local copies, waits for them, and re-layouts, advance(): return jnp.stack([new_re, new_im], axis=0)  2.59 us
    squeeze x3, local copies, waits for them, and re-layouts, advance(): other_im = partner[1]  1.99 us
    unnamed x3, local copies, waits for them, and re-layouts  1.89 us
    neg x3, other arithmetic, advance(): -other_im  1.85 us
  transfers between devices with their start and end apart: 3, of which 3 were waited for; matrix products, arithmetic and copies ran while one was open for 4% of the time, Pallas kernels for 0%

profile of v1, /device:TPU:1, one launch (start us, length us, event | category | flops | bytes accessed | tf_op | source)
XLA Modules:
  0.0 68.2 jit_solution(909643725803198252)
XLA Ops:
  0.0 1.9 %copy.8 = f32[1,2,64,256]{2,3,1,0:T(8,128)} copy(f32[1,2,64,256]{3,2,1,0:T(8,128)} %param.2) | data formatting | bytes 262144 | tf_op args[0]
  1.9 5.7 %collective-permute-start = (f32[2,64,16,16]{1,3,2,0:T(8,128)}, f32[2,64,16,16]{1,3,2,0:T(8,128)}, u32[]{:S(2)}, u32[]{:S(2)}) collective-permute-start(f32[2,64,16,16]{1,3,2,0:T(8,128)} %bitcast.2), channel_id=1, source_target_pairs={{0,64},{4,68},{8,72},{12,76},{16,80},{20,84},{24,88},{28,92},{32,9... | collective-permute-start | bytes 393224 | tf_op jit(solution)/shard_map/ppermute | solution.py:12
  7.6 1.5 %fusion.69 = (f32[1,1,64,256]{3,2,1,0:T(8,128)S(1)}, f32[1,1,64,256]{3,2,1,0:T(8,128)}) fusion(f32[1,2,64,256]{3,2,1,0:T(8,128)} %param.2), kind=kLoop, calls=%fused_computation.81 | loop fusion | bytes 262144 | tf_op jit(solution)/shard_map/slice | solution.py:21
  9.2 0.9 %copy.6 = f32[1,1,64,256]{2,3,1,0:T(8,128)S(1)} copy(f32[1,1,64,256]{3,2,1,0:T(8,128)} %get-tuple-element.12) | data formatting | bytes 131072 | tf_op jit(solution)/shard_map/slice | solution.py:20
  10.2 8.7 %collective-permute-done = f32[2,64,16,16]{1,3,2,0:T(8,128)} collective-permute-done((f32[2,64,16,16]{1,3,2,0:T(8,128)}, f32[2,64,16,16]{1,3,2,0:T(8,128)}, u32[]{:S(2)}, u32[]{:S(2)}) %collective-permute-start) | collective-permute-done | bytes 131104 | tf_op jit(solution)/shard_map/ppermute | solution.py:12
  18.9 1.0 %slice_bitcast_fusion.4 = (f32[64,16,16]{0,2,1:T(8,128)S(1)}, f32[64,16,16]{0,2,1:T(8,128)S(1)}) fusion(f32[2,64,16,16]{1,3,2,0:T(8,128)} %collective-permute-done), kind=kLoop, calls=%fused_computation.66 | loop fusion | bytes 262144 | tf_op jit(solution)/shard_map/squeeze | solution.py:24
  19.9 2.3 %bitcast_negate_fusion.1 = (f32[64,16,16]{0,2,1:T(8,128)S(1)}, f32[16,16,64]{2,1,0:T(8,128)S(1)}) fusion(f32[1,3,16,64,256]{4,3,2,1,0:T(8,128)} %param.3, f32[64,16,16]{0,2,1:T(8,128)S(1)} %get-tuple-element.10, f32[64,16,16]{0,2,1:T(8,128)S(1)} %get-tuple-element.9, f32[64,16,16]{0,2,1:T(8,128)S(1)} %bitcast.70, f32[64,16,16]{0,2,1:T(8,128)S(1)} %bitcast.69), kind=kOutput, calls=%fused_computation.77 | convolution fusion | flops 50544640 | bytes 1441792 | tf_op jit(solution)/shard_map/boj,jbk->obk/dot_general | solution.py:16
  22.1 0.9 %fusion.66 = f32[64,16,16]{0,2,1:T(8,128)S(1)} fusion(f32[2,64,16,16]{1,3,2,0:T(8,128)} %collective-permute-done), kind=kLoop, calls=%fused_computation.78 | loop fusion | flops 16384 | bytes 131072 | tf_op jit(solution)/shard_map/neg | solution.py:25
  23.1 1.1 %fusion.10 = f32[16,16,64]{2,1,0:T(8,128)S(1)} fusion(f32[1,3,16,64,256]{4,3,2,1,0:T(8,128)S(1)} %copy-done, f32[64,16,16]{0,2,1:T(8,128)S(1)} %fusion.66, f32[64,16,16]{0,2,1:T(8,128)S(1)} %get-tuple-element.10, f32[64,16,16]{0,2,1:T(8,128)S(1)} %neg.18, f32[64,16,16]{0,2,1:T(8,128)S(1)} %bitcast.71), kind=kOutput, calls=%fused_computation.10 | convolution fusion | flops 50528256 | bytes 1638400 | tf_op jit(solution)/shard_map/boj,jbk->obk/dot_general | solution.py:16
  24.2 3.8 %collective-permute-start.1 = (f32[2,64,16,16]{1,3,2,0:T(8,128)S(1)}, f32[2,64,16,16]{1,3,2,0:T(8,128)S(1)}, u32[]{:S(2)}, u32[]{:S(2)}) collective-permute-start(f32[2,64,16,16]{1,3,2,0:T(8,128)S(1)} %pad_maximum_fusion), channel_id=1, source_target_pairs={{0,32},{4,36},{8,40},{12,44},{16,48},{20,52},{24,56},{28,60},{32,0... | collective-permute-start | bytes 393224 | tf_op jit(solution)/shard_map/ppermute | solution.py:12
  27.9 5.2 %collective-permute-done.1 = f32[2,64,16,16]{1,3,2,0:T(8,128)S(1)} collective-permute-done((f32[2,64,16,16]{1,3,2,0:T(8,128)S(1)}, f32[2,64,16,16]{1,3,2,0:T(8,128)S(1)}, u32[]{:S(2)}, u32[]{:S(2)}) %collective-permute-start.1) | collective-permute-done | bytes 131104 | tf_op jit(solution)/shard_map/ppermute | solution.py:12
  33.1 1.1 %fusion.6 = f32[16,16,64]{2,1,0:T(8,128)S(1)} fusion(f32[1,3,16,64,256]{4,3,2,1,0:T(8,128)S(1)} %copy-done, f32[64,16,16]{0,2,1:T(8,128)S(1)} %fusion.67, f32[64,16,16]{0,2,1:T(8,128)S(1)} %get-tuple-element.8, f32[64,16,16]{0,2,1:T(8,128)S(1)} %get-tuple-element.13, f32[64,16,16]{0,2,1:T(8,128)S(1)} %bitcast.61), kind=kOutput, calls=%fused_computation.6 | convolution fusion | flops 50528256 | bytes 1638400 | tf_op jit(solution)/shard_map/boj,jbk->obk/dot_general | solution.py:16
  34.2 1.7 %bitcast_negate_fusion = (f32[64,16,16]{0,2,1:T(8,128)}, f32[16,16,64]{2,1,0:T(8,128)S(1)}) fusion(f32[1,3,16,64,256]{4,3,2,1,0:T(8,128)S(1)} %copy-done, f32[64,16,16]{0,2,1:T(8,128)S(1)} %get-tuple-element.8, f32[64,16,16]{0,2,1:T(8,128)S(1)} %get-tuple-element.7, f32[64,16,16]{0,2,1:T(8,128)S(1)} %bitcast.62, f32[64,16,16]{0,2,1:T(8,128)S(1)} %bitcast.67), kind=kOutput, calls=%fused_computation.76 | convolution fusion | flops 50544640 | bytes 1703936 | tf_op jit(solution)/shard_map/boj,jbk->obk/dot_general | solution.py:16
  35.9 0.7 %pad_maximum_fusion.1 = f32[2,64,16,16]{1,3,2,0:T(8,128)} fusion(f32[1,64,16,16]{1,3,2,0:T(8,128)S(1)} %bitcast.72, f32[1,64,16,16]{1,3,2,0:T(8,128)S(1)} %bitcast.63), kind=kLoop, calls=%fused_computation.47 | loop fusion | flops 32768 | bytes 262144 | tf_op jit(solution)/shard_map/stack | solution.py:29
  36.6 5.0 %collective-permute-start.2 = (f32[2,64,16,16]{1,3,2,0:T(8,128)}, f32[2,64,16,16]{1,3,2,0:T(8,128)}, u32[]{:S(2)}, u32[]{:S(2)}) collective-permute-start(f32[2,64,16,16]{1,3,2,0:T(8,128)} %pad_maximum_fusion.1), channel_id=1, source_target_pairs={{0,16},{4,20},{8,24},{12,28},{16,0},{20,4},{24,8},{28,12},{32,48},... | collective-permute-start | bytes 393224 | tf_op jit(solution)/shard_map/ppermute | solution.py:12
  41.7 4.7 %collective-permute-done.2 = f32[2,64,16,16]{1,3,2,0:T(8,128)} collective-permute-done((f32[2,64,16,16]{1,3,2,0:T(8,128)}, f32[2,64,16,16]{1,3,2,0:T(8,128)}, u32[]{:S(2)}, u32[]{:S(2)}) %collective-permute-start.2) | collective-permute-done | bytes 131104 | tf_op jit(solution)/shard_map/ppermute | solution.py:12
  46.4 1.0 %slice_bitcast_fusion = (f32[64,16,16]{0,2,1:T(8,128)S(1)}, f32[64,16,16]{0,2,1:T(8,128)S(1)}) fusion(f32[2,64,16,16]{1,3,2,0:T(8,128)} %collective-permute-done.2), kind=kLoop, calls=%fused_computation.62 | loop fusion | bytes 262144 | tf_op jit(solution)/shard_map/squeeze | solution.py:24
  47.4 1.7 %fusion = f32[16,16,64]{2,1,0:T(8,128)} fusion(f32[1,3,16,64,256]{4,3,2,1,0:T(8,128)S(1)} %copy-done, f32[64,16,16]{0,2,1:T(8,128)S(1)} %get-tuple-element.6, f32[64,16,16]{0,2,1:T(8,128)S(1)} %get-tuple-element.5, f32[64,16,16]{0,2,1:T(8,128)S(1)} %bitcast.64, f32[64,16,16]{0,2,1:T(8,128)S(1)} %bitcast.73), kind=kOutput, calls=%fused_computation | convolution fusion | flops 50528256 | bytes 1638400 | tf_op jit(solution)/shard_map/boj,jbk->obk/dot_general | solution.py:16
  49.1 1.6 %copy.10 = f32[1,1,64,256]{3,2,1,0:T(8,128)} copy(f32[1,1,64,256]{2,3,1,0:T(8,128)} %bitcast.75) | data formatting | bytes 131072 | tf_op jit(solution)/shard_map/stack | solution.py:29
  50.7 0.9 %fusion.68 = f32[64,16,16]{0,2,1:T(8,128)S(1)} fusion(f32[2,64,16,16]{1,3,2,0:T(8,128)} %collective-permute-done.2), kind=kLoop, calls=%fused_computation.80 | loop fusion | flops 16384 | bytes 131072 | tf_op jit(solution)/shard_map/neg | solution.py:25
  51.6 2.6 %fusion.2 = f32[16,16,64]{2,1,0:T(8,128)} fusion(f32[1,3,16,64,256]{4,3,2,1,0:T(8,128)S(1)} %copy-done, f32[64,16,16]{0,2,1:T(8,128)S(1)} %fusion.68, f32[64,16,16]{0,2,1:T(8,128)S(1)} %get-tuple-element.6, f32[64,16,16]{0,2,1:T(8,128)} %get-tuple-element.15, f32[64,16,16]{0,2,1:T(8,128)S(1)} %bitcast.65), kind=kOutput, calls=%fused_computation.2 | convolution fusion | flops 50528256 | bytes 1572864 | tf_op jit(solution)/shard_map/boj,jbk->obk/dot_general | solution.py:16
  54.2 1.0 %copy.9 = f32[1,1,64,256]{3,2,1,0:T(8,128)S(1)} copy(f32[1,1,64,256]{2,3,1,0:T(8,128)} %bitcast.74) | data formatting | bytes 131072 | tf_op jit(solution)/shard_map/stack | solution.py:29
  55.2 0.8 %pad_maximum_fusion.2 = f32[1,2,64,256]{3,2,1,0:T(8,128)S(1)} fusion(f32[1,1,64,256]{3,2,1,0:T(8,128)} %copy.10, f32[1,1,64,256]{3,2,1,0:T(8,128)S(1)} %copy.9), kind=kLoop, calls=%fused_computation.68 | loop fusion | flops 32768 | bytes 262144 | tf_op jit(solution)/shard_map/stack | solution.py:29
  56.1 11.4 %all_gather.3 = f32[4,2,64,256]{3,2,1,0:T(8,128)S(1)} all-gather(f32[1,2,64,256]{3,2,1,0:T(8,128)S(1)} %pad_maximum_fusion.2), channel_id=1, replica_groups=mesh['bis'=128,'src'=4] {'src'}, dimensions={0}, use_global_device_ids=true | all-gather | bytes 655360 | tf_op jit(solution)/shard_map/all_gather | solution.py:41
  (9 shorter events, 0.8 us)
Async XLA Ops:
  0.0 23.1 %copy-start = (f32[1,3,16,64,256]{4,3,2,1,0:T(8,128)S(1)}, f32[1,3,16,64,256]{4,3,2,1,0:T(8,128)}, u32[]{:S(2)}) copy-start(f32[1,3,16,64,256]{4,3,2,1,0:T(8,128)} %param.3) | copy-start | bytes 9437188
  1.9 17.0 %collective-permute-start = (f32[2,64,16,16]{1,3,2,0:T(8,128)}, f32[2,64,16,16]{1,3,2,0:T(8,128)}, u32[]{:S(2)}, u32[]{:S(2)}) collective-permute-start(f32[2,64,16,16]{1,3,2,0:T(8,128)} %bitcast.2), channel_id=1, source_target_pairs={{0,64},{4,68},{8,72},{12,76},{16,80},{20,84},{24,88},{28,92},{32,9... | collective-permute-start | bytes 393224 | tf_op jit(solution)/shard_map/ppermute | solution.py:12
  24.2 8.9 %collective-permute-start.1 = (f32[2,64,16,16]{1,3,2,0:T(8,128)S(1)}, f32[2,64,16,16]{1,3,2,0:T(8,128)S(1)}, u32[]{:S(2)}, u32[]{:S(2)}) collective-permute-start(f32[2,64,16,16]{1,3,2,0:T(8,128)S(1)} %pad_maximum_fusion), channel_id=1, source_target_pairs={{0,32},{4,36},{8,40},{12,44},{16,48},{20,52},{24,56},{28,60},{32,0... | collective-permute-start | bytes 393224 | tf_op jit(solution)/shard_map/ppermute | solution.py:12
  36.6 9.8 %collective-permute-start.2 = (f32[2,64,16,16]{1,3,2,0:T(8,128)}, f32[2,64,16,16]{1,3,2,0:T(8,128)}, u32[]{:S(2)}, u32[]{:S(2)}) collective-permute-start(f32[2,64,16,16]{1,3,2,0:T(8,128)} %pad_maximum_fusion.1), channel_id=1, source_target_pairs={{0,16},{4,20},{8,24},{12,28},{16,0},{20,4},{24,8},{28,12},{32,48},... | collective-permute-start | bytes 393224 | tf_op jit(solution)/shard_map/ppermute | solution.py:12
